TPU v7x, 32 devices: a whole 2x2x4 slice. The times are simulated.
32 devices in a mesh: tm: 4 (over y, x), tile: 8 (over z, core).
Axes of the slice: x: 2, y: 2, z: 4, core: 2. Of those that a mesh axis runs over, the one named last changes fastest.
Arguments:
- diag_blocks: float32 [16384, 4096], P(('tm', 'tile')), as said below
- coupling: float32 [16384, 4096], P(('tm', 'tile')), as said below
- next_diag: float32 [16384, 4096], P(('tm', 'tile')), as said below
- arrow_now: float32 [128, 4096], P('tm'), may hold values from -0.4375 to 0.4375
- arrow_next: float32 [128, 4096], P('tm'), may hold values from -0.4375 to 0.4375
- arrow_tip: float32 [128, 32], P('tm'), may hold values from -6 to 6
Outputs:
- factor_lower: float32 [16384, 4096], P(('tm', 'tile'))
- coupling_out: float32 [16384, 4096], P(('tm', 'tile'))
- arrow_factor: float32 [128, 4096], P('tm')
- handed_diag: float32 [16384, 4096], P(('tm', 'tile'))
- handed_arrow: float32 [128, 4096], P('tm')
- handed_tip: float32 [128, 32], P('tm')
Inputs may be any that keep to these rules, and one draw needn't show every extreme that they name: `diag_blocks`: each 4096 x 4096 block is symmetric positive definite. `next_diag`: each 4096 x 4096 block is symmetric positive definite. `coupling`: with the diag_blocks block and the next_diag block of its time step, each 4096 x 4096 block forms a symmetric positive definite two-block precision matrix.
All inputs are finite; a program needn't handle non-finite values.
Results may differ from a plain program's by a relative error of at most 0.0001.
Values sent between devices are 32-bit elements; how exact they have to be, the bound alone decides.
No kernel may reach another device: no remote copies, remote signals or barrier semaphores. Data moves between devices by JAX's collectives and lax.ppermute only.
A program may use at most 256 MiB of HBM per device.

v0:
```python
import jax
import jax.numpy as jnp
from jax import lax
from jax.sharding import PartitionSpec as P

precise = lax.Precision.HIGHEST


def broadcast(block, axis, source):
    block = jnp.where(lax.axis_index(axis) == source, block, jnp.zeros_like(block))
    return lax.psum(block, axis)


def shifted(value, axis, steps):
    count = lax.axis_size(axis)
    leading, last = (max(0, -steps), min(count, count - steps))
    return lax.ppermute(value, axis, [(source, source + steps) for source in range(leading, last)])


def outer_rows(left_rows, right_rows):
    return lax.dot_general(
        left_rows,
        right_rows,
        (((1,), (1,)), ((), ())),
        precision=precise,
        preferred_element_type=jnp.float32,
    )


def solve_rows(factor, block):
    return jax.scipy.linalg.solve_triangular(factor, block.T, lower=True).T


def local(diag_blocks, coupling, next_diag, arrow_now, arrow_next, arrow_tip):
    row_count = diag_blocks.shape[0]
    col_count = diag_blocks.shape[1]
    panels = lax.axis_size("tile") // 4
    my_index = lax.axis_index("tile")
    row_ids = my_index * row_count + lax.iota(jnp.int32, row_count)
    work_a, work_c, arrow_a = (diag_blocks, coupling, arrow_now)
    next_d, arrow_b, tip_block = (next_diag, arrow_next, arrow_tip)
    for number in range(panels):
        offset = number * row_count
        factor_offset = number * row_count
        factor_ending = factor_offset + row_count
        pivot_blk = broadcast(work_a[:, factor_offset:factor_ending], "tile", number)
        factor = jnp.linalg.cholesky(pivot_blk)
        factor_local_a = jnp.where(
            (row_ids >= factor_offset)[:, None],
            solve_rows(factor, work_a[:, factor_offset:factor_ending]),
            0.0,
        )
        factor_local_c = solve_rows(factor, work_c[:, factor_offset:factor_ending])
        factor_whole_a = lax.all_gather(factor_local_a, "tile", axis=0, tiled=True)
        factor_whole_c = lax.all_gather(factor_local_c, "tile", axis=0, tiled=True)
        factor_local_r = solve_rows(factor, arrow_a[:, factor_offset:factor_ending])
        panel_k = (
            factor_offset,
            factor_local_a,
            factor_local_c,
            factor_local_r,
            factor_whole_a,
            factor_whole_c,
        )
        store_work_a = work_a
        store_work_c = work_c
        store_arrow_a = arrow_a
        store_offset = panel_k[0]
        store_local_a = panel_k[1]
        store_local_c = panel_k[2]
        store_local_r = panel_k[3]
        ending = store_offset + row_count
        store_work_a = store_work_a.at[:, store_offset:ending].set(store_local_a)
        store_work_c = store_work_c.at[:, store_offset:ending].set(store_local_c)
        store_arrow_a = store_arrow_a.at[:, store_offset:ending].set(store_local_r)
        work_a = store_work_a
        work_c = store_work_c
        arrow_a = store_arrow_a
        col_lo = offset + row_count
        apply_work_a = work_a
        apply_work_c = work_c
        apply_arrow_a = arrow_a
        apply_offset = panel_k[0]
        local_a = panel_k[1]
        apply_local_c = panel_k[2]
        apply_local_r = panel_k[3]
        whole_a = panel_k[4]
        keep_rows = (row_ids >= apply_offset + row_count)[:, None]
        targets = whole_a[col_lo:col_count]
        apply_work_a = apply_work_a.at[:, col_lo:col_count].add(
            -jnp.where(keep_rows, outer_rows(local_a, targets), 0.0)
        )
        apply_work_c = apply_work_c.at[:, col_lo:col_count].add(-outer_rows(apply_local_c, targets))
        apply_arrow_a = apply_arrow_a.at[:, col_lo:col_count].add(
            -outer_rows(apply_local_r, targets)
        )
        work_a = apply_work_a
        work_c = apply_work_c
        arrow_a = apply_arrow_a
        apply_next_d = next_d
        apply_arrow_b = arrow_b
        apply_tip_block = tip_block
        local_c = panel_k[2]
        local_r = panel_k[3]
        whole_c = panel_k[5]
        apply_next_d = apply_next_d - outer_rows(local_c, whole_c)
        apply_arrow_b = apply_arrow_b - outer_rows(local_r, whole_c)
        apply_tip_block = apply_tip_block - outer_rows(local_r, local_r)
        next_d = apply_next_d
        arrow_b = apply_arrow_b
        tip_block = apply_tip_block
    col_ids = lax.iota(jnp.int32, col_count)
    factor_lower = jnp.where(col_ids[None, :] <= row_ids[:, None], work_a, 0.0)
    handed_diag, handed_arrow, handed_tip = shifted((next_d, arrow_b, tip_block), "tm", 1)
    return (factor_lower, work_c, arrow_a, handed_diag, handed_arrow, handed_tip)


def solution(mesh):
    return jax.shard_map(
        local,
        mesh=mesh,
        in_specs=(
            P(("tm", "tile"), None),
            P(("tm", "tile"), None),
            P(("tm", "tile"), None),
            P("tm", None),
            P("tm", None),
            P("tm", None),
        ),
        out_specs=(
            P(("tm", "tile"), None),
            P(("tm", "tile"), None),
            P("tm", None),
            P(("tm", "tile"), None),
            P("tm", None),
            P("tm", None),
        ),
        check_vma=False,
    )
```

profile of v0, /device:TPU:0, one launch (start us, length us, event | category | flops | bytes accessed | tf_op | source)
XLA Modules:
  0.0 914.3 jit_solution(8446192928893483997)
XLA Ops:
  22.5 61.0 %all-reduce.4.cloned.1.call-done = f32[512,512]{1,0:T(8,128)} async-done(((f32[512,512]{1,0:T(8,128)}), f32[512,512]{1,0:T(8,128)}) %all-reduce.4.cloned.1.call-update) | async-done | bytes 1048592 | tf_op jit(solution)/shard_map/psum | solution.py:11
  86.6 11.7 %cholesky.286 = f32[128,128]{1,0:T(8,128)S(1)} custom-call(f32[128,128]{1,0:T(8,128)S(1)} %copy.14), custom_call_target="Cholesky" | custom-call | tf_op jit(solution)/shard_map/jit(cholesky)/cholesky | solution.py:47
  109.3 11.7 %cholesky.305 = f32[128,128]{1,0:T(8,128)S(1)} custom-call(f32[128,128]{1,0:T(8,128)S(1)} %copy.16), custom_call_target="Cholesky" | custom-call | tf_op jit(solution)/shard_map/jit(cholesky)/cholesky | solution.py:47
  121.1 10.0 %custom-call.34 = f32[1,128,128]{1,2,0:T(8,128)S(1)} custom-call(f32[1,128,128]{2,1,0:T(8,128)S(1)} %get-tuple-element.243), custom_call_target="InvertDiagBlocksLowerTriangular" | custom-call | tf_op jit(solution)/shard_map/jit(cholesky)/cholesky | solution.py:47
  132.0 11.7 %cholesky.326 = f32[128,128]{1,0:T(8,128)S(1)} custom-call(f32[128,128]{1,0:T(8,128)S(1)} %copy.18), custom_call_target="Cholesky" | custom-call | tf_op jit(solution)/shard_map/jit(cholesky)/cholesky | solution.py:47
  155.0 12.2 %cholesky.343 = f32[128,128]{1,0:T(8,128)S(1)} custom-call(f32[128,128]{1,0:T(8,128)S(1)} %copy.20), custom_call_target="Cholesky" | custom-call | tf_op jit(solution)/shard_map/jit(cholesky)/cholesky | solution.py:47
  178.9 39.3 %custom-call.36 = f32[4,128,128]{1,2,0:T(8,128)S(1)} custom-call(f32[4,128,128]{2,1,0:T(8,128)S(1)} %get-tuple-element.193), custom_call_target="InvertDiagBlocksLowerTriangular" | custom-call | tf_op jit(solution)/shard_map/jit(_solve_triangular)/triangular_solve | solution.py:31
  237.6 73.9 %all-gather.5.cloned.1.call-done = f32[4096,512]{1,0:T(8,128)} async-done(((f32[512,512]{1,0:T(8,128)}), f32[4096,512]{1,0:T(8,128)}) %all-gather.5.cloned.1.call-update) | async-done | bytes 8388624 | tf_op jit(solution)/shard_map/all_gather | solution.py:54
  311.4 17.8 %constant_dynamic-update-slice_fusion.4 = (f32[512,4096]{1,0:T(8,128)}, f32[512,3584]{1,0:T(8,128)S(1)}) fusion(f32[512,4096]{1,0:T(8,128)} %get-tuple-element.217, f32[4096,512]{1,0:T(8,128)} %all-gather.5.cloned.1.call-done, f32[128,512]{0,1:T(8,128)} %copy-done.17, f32[128,512]{0,1:T(8,128)} %copy-done.16, f32[128,512]{0,1:T(8,128)} %copy-done.15, ...), kind=kOutput, calls=%fused_computation.244 | convolution fusion | flops 11280842752 | bytes 30409728 | tf_op jit(solution)/shard_map/dot_general | solution.py:21
  344.0 17.6 %constant_dynamic-update-slice_fusion.3 = (f32[512,4096]{1,0:T(8,128)}, f32[512,3584]{1,0:T(8,128)S(1)}) fusion(f32[512,4096]{1,0:T(8,128)} %select_dynamic-update-slice_fusion.1, f32[4096,512]{1,0:T(8,128)} %all-gather.5.cloned.1.call-done, f32[128,512]{0,1:T(8,128)S(1)} %fusion.130, f32[128,512]{0,1:T(8,128)S(1)} %copy.33, f32[128,512]{0,1:T(8,128)S(1)} %copy.32, ...), kind=kOutput, calls=%fused_computation.243 | convolution fusion | flops 11278745600 | bytes 30408704 | tf_op jit(solution)/shard_map/dot_general | solution.py:21
  365.6 28.9 %all-reduce.6.cloned.1.call-done = f32[512,512]{0,1:T(8,128)} async-done(((f32[512,512]{0,1:T(8,128)}), f32[512,512]{0,1:T(8,128)}) %all-reduce.6.cloned.1.call-update) | async-done | bytes 1048592 | tf_op jit(solution)/shard_map/psum | solution.py:11
  398.5 11.7 %cholesky.358 = f32[128,128]{1,0:T(8,128)S(1)} custom-call(f32[128,128]{1,0:T(8,128)S(1)} %cholesky.439), custom_call_target="Cholesky" | custom-call | tf_op jit(solution)/shard_map/jit(cholesky)/cholesky | solution.py:47
  423.4 11.7 %cholesky.377 = f32[128,128]{1,0:T(8,128)S(1)} custom-call(f32[128,128]{1,0:T(8,128)S(1)} %cholesky.443), custom_call_target="Cholesky" | custom-call | tf_op jit(solution)/shard_map/jit(cholesky)/cholesky | solution.py:47
  435.1 9.9 %custom-call.38 = f32[1,128,128]{1,2,0:T(8,128)S(1)} custom-call(f32[1,128,128]{2,1,0:T(8,128)S(1)} %get-tuple-element.233), custom_call_target="InvertDiagBlocksLowerTriangular" | custom-call | tf_op jit(solution)/shard_map/jit(cholesky)/cholesky | solution.py:47
  447.5 11.7 %cholesky.398 = f32[128,128]{1,0:T(8,128)S(1)} custom-call(f32[128,128]{1,0:T(8,128)S(1)} %cholesky.448), custom_call_target="Cholesky" | custom-call | tf_op jit(solution)/shard_map/jit(cholesky)/cholesky | solution.py:47
  470.5 11.7 %cholesky.415 = f32[128,128]{1,0:T(8,128)S(1)} custom-call(f32[128,128]{1,0:T(8,128)S(1)} %convolution_subtract_fusion.18), custom_call_target="Cholesky" | custom-call | tf_op jit(solution)/shard_map/jit(cholesky)/cholesky | solution.py:47
  488.9 11.9 %while.25 = (s32[]{:T(128)}, f32[512,512]{1,0:T(8,128)}, s32[4,2]{0,1:T(2,128)S(1)}, f32[4,128,128]{2,1,0:T(8,128)S(1)}, s32[]{:T(128)}) while((s32[]{:T(128)}, f32[512,512]{1,0:T(8,128)}, s32[4,2]{0,1:T(2,128)S(1)}, f32[4,128,128]{2,1,0:T(8,128)S(1)}, s32[]{:T(128)}) %tuple.143), condition=%wide.while_cond.12.clone, body=%wide.while_body.12.clone.sunk | while | flops 2 | bytes 131189 | solution.py:31
  500.8 39.3 %custom-call.40 = f32[4,128,128]{1,2,0:T(8,128)S(1)} custom-call(f32[4,128,128]{2,1,0:T(8,128)S(1)} %get-tuple-element.194), custom_call_target="InvertDiagBlocksLowerTriangular" | custom-call | tf_op jit(solution)/shard_map/jit(_solve_triangular)/triangular_solve | solution.py:31
  579.8 17.3 %fusion.92 = f32[512,4096]{1,0:T(8,128)} fusion(f32[4096,512]{1,0:T(8,128)} %all-gather.9.cloned.1.call-done, f32[128,512]{0,1:T(8,128)S(1)} %fusion.130, f32[128,512]{0,1:T(8,128)S(1)} %copy.33, f32[128,512]{0,1:T(8,128)S(1)} %copy.32, f32[128,512]{0,1:T(8,128)S(1)} %copy.31), kind=kOutput, calls=%fused_computation.136 | convolution fusion | flops 12885688320 | bytes 17825792 | tf_op jit(solution)/shard_map/dot_general | solution.py:21
  597.0 37.2 %all-gather.11.cloned.1.call-done = f32[4096,512]{1,0:T(8,128)} async-done(((f32[512,512]{1,0:T(8,128)}), f32[4096,512]{1,0:T(8,128)}) %all-gather.11.cloned.1.call-update) | async-done | bytes 8388624 | tf_op jit(solution)/shard_map/all_gather | solution.py:55
  634.2 21.0 %subtract_subtract_fusion = f32[512,4096]{1,0:T(8,128)} fusion(f32[512,4096]{1,0:T(8,128)} %param.37, f32[512,4096]{1,0:T(8,128)} %fusion.92, f32[4096,512]{1,0:T(8,128)} %all-gather.11.cloned.1.call-done, f32[128,512]{0,1:T(8,128)S(1)} %fusion.140, f32[128,512]{0,1:T(8,128)S(1)} %copy.37, f32[128,512]{0,1:T(8,128)S(1)} %copy.36, f32[128,512]{0,1:T(8,128)S(1)} %copy.35), kind=kOutput, calls=%fused_computation.4 | convolution fusion | flops 12889882624 | bytes 34603008 | tf_op jit(solution)/shard_map/dot_general | solution.py:21
  690.5 149.0 %collective-permute-done.2 = f32[32,32]{1,0:T(8,128)S(1)} collective-permute-done((f32[32,32]{1,0:T(8,128)S(1)}, f32[32,32]{1,0:T(8,128)S(1)}, u32[]{:S(2)}, u32[]{:S(2)}) %collective-permute-start.2) | collective-permute-done | bytes 4128 | tf_op jit(solution)/shard_map/ppermute | solution.py:17
  852.7 15.2 %fusion.7 = f32[512,4096]{1,0:T(8,128)} fusion(f32[512,4096]{1,0:T(8,128)} %get-tuple-element.215, f32[4096,512]{1,0:T(8,128)} %all-gather.7.cloned.1.call-done, pred[512]{0:T(512)(128)(4,1)S(1)} %fusion.166, f32[128,512]{0,1:T(8,128)S(1)} %copy-done.13, f32[128,512]{0,1:T(8,128)S(1)} %copy-done.11, f32[128,512]{0,1:T(8,128)S(1)} %copy-done.10, ...), kind=kOutput, calls=%fused_computation.17 | convolution fusion | flops 9669443584 | bytes 19923968 | tf_op jit(solution)/shard_map/dot_general | solution.py:21
  876.7 14.0 %fusion.6 = f32[512,4096]{1,0:T(8,128)} fusion(f32[512,4096]{1,0:T(8,128)} %select_dynamic-update-slice_fusion, f32[4096,512]{1,0:T(8,128)S(1)} %copy-done, f32[128,512]{0,1:T(8,128)S(1)} %fusion.140, f32[128,512]{0,1:T(8,128)S(1)} %copy.37, f32[128,512]{0,1:T(8,128)S(1)} %copy.36, f32[128,512]{0,1:T(8,128)S(1)} %copy.35), kind=kOutput, calls=%fused_computation.15 | convolution fusion | flops 9667608576 | bytes 19922944 | tf_op jit(solution)/shard_map/dot_general | solution.py:21
  (246 shorter events, 255.4 us)
Async XLA Ops:
  7.2 76.3 %all-reduce.4.cloned.1.call-start = ((), (), s32[]{:S(2)}) async-start(), calls=%async_computation | async-start | bytes 2097152 | tf_op jit(solution)/shard_map/psum | solution.py:11
  21.8 289.6 %all-gather.5.cloned.1.call-start = ((), (), s32[]{:S(2)}) async-start(), calls=%async_computation.1 | async-start | bytes 9437184 | tf_op jit(solution)/shard_map/all_gather | solution.py:54
  218.8 11.5 %copy-start.14 = (f32[128,512]{0,1:T(8,128)}, f32[128,512]{0,1:T(8,128)S(1)}, u32[]{:S(2)}) copy-start(f32[128,512]{0,1:T(8,128)S(1)} %copy.21) | copy-start | bytes 786436
  219.9 10.4 %copy-start.15 = (f32[128,512]{0,1:T(8,128)}, f32[128,512]{0,1:T(8,128)S(1)}, u32[]{:S(2)}) copy-start(f32[128,512]{0,1:T(8,128)S(1)} %copy.22) | copy-start | bytes 786436
  230.3 164.2 %all-reduce.6.cloned.1.call-start = ((), (), s32[]{:S(2)}) async-start(), calls=%async_computation.2 | async-start | bytes 2097152 | tf_op jit(solution)/shard_map/psum | solution.py:11
  231.7 97.6 %copy-start.7 = (f32[512,512]{0,1:T(8,128)}, f32[512,512]{0,1:T(8,128)S(1)}, u32[]{:S(2)}) copy-start(f32[512,512]{0,1:T(8,128)S(1)} %slice_bitcast_fusion.1) | copy-start | bytes 3145732
  336.1 243.6 %all-gather.9.cloned.1.call-start = ((), (), s32[]{:S(2)}) async-start(), calls=%async_computation.4 | async-start | bytes 9437184 | tf_op jit(solution)/shard_map/all_gather | solution.py:55
  341.0 293.2 %all-gather.11.cloned.1.call-start = ((), (), s32[]{:S(2)}) async-start(), calls=%async_computation.5 | async-start | bytes 9437184 | tf_op jit(solution)/shard_map/all_gather | solution.py:55
  553.1 299.6 %all-gather.7.cloned.1.call-start = ((), (), s32[]{:S(2)}) async-start(), calls=%async_computation.3 | async-start | bytes 9437184 | tf_op jit(solution)/shard_map/all_gather | solution.py:54
  597.0 66.1 %copy-start.26 = (f32[32,32]{1,0:T(8,128)S(1)}, f32[32,32]{1,0:T(8,128)}, u32[]{:S(2)}) copy-start(f32[32,32]{1,0:T(8,128)} %param.40) | copy-start | bytes 12292
  597.0 66.3 %copy-start.5 = (f32[32,4096]{1,0:T(8,128)S(1)}, f32[32,4096]{1,0:T(8,128)}, u32[]{:S(2)}) copy-start(f32[32,4096]{1,0:T(8,128)} %copy.107) | copy-start | bytes 1572868
  655.2 18.1 %copy-start.1 = (f32[4096,512]{1,0:T(8,128)S(1)}, f32[4096,512]{1,0:T(8,128)}, u32[]{:S(2)}) copy-start(f32[4096,512]{1,0:T(8,128)} %all-gather.9.cloned.1.call-done) | copy-start | bytes 25165828
  655.2 18.1 %copy-start.24 = (f32[32,4096]{1,0:T(8,128)S(1)}, f32[32,4096]{1,0:T(8,128)}, u32[]{:S(2)}) copy-start(f32[32,4096]{1,0:T(8,128)} %param.39) | copy-start | bytes 1572868
  655.2 241.3 %collective-permute-start = (f32[512,4096]{1,0:T(8,128)}, f32[512,4096]{1,0:T(8,128)}, u32[]{:S(2)}, u32[]{:S(2)}) collective-permute-start(f32[512,4096]{1,0:T(8,128)} %subtract_subtract_fusion), channel_id=1, source_target_pairs={{0,8},{8,16},{16,24},{1,9},{9,17},{17,25},{2,10},{10,18},{18,26},{... | collective-permute-start | bytes 25165832 | tf_op jit(solution)/shard_map/ppermute | solution.py:17
  664.0 17.0 %copy-start.21 = (f32[4,128,128]{1,2,0:T(8,128)S(1)}, f32[4,128,128]{1,2,0:T(8,128)}, u32[]{:S(2)}) copy-start(f32[4,128,128]{1,2,0:T(8,128)} %copy-done.20) | copy-start | bytes 786436
  664.0 175.5 %slice-start = ((s8[8388608]{0:T(1024)(128)(4,1)}), s8[4194304]{0:T(1024)(128)(4,1)S(1)}, s32[]{:S(2)}) async-start(s8[8388608]{0:T(1024)(128)(4,1)} %bitcast.194), calls=%async_computation.6 | async-start | bytes 8388608
  673.4 166.2 %slice-start.1 = ((s8[8388608]{0:T(1024)(128)(4,1)}), s8[4194304]{0:T(1024)(128)(4,1)S(1)}, s32[]{:S(2)}) async-start(s8[8388608]{0:T(1024)(128)(4,1)} %bitcast.194), calls=%async_computation.7 | async-start | bytes 8388608
  681.0 171.7 %copy-start.9 = (f32[128,512]{0,1:T(8,128)S(1)}, f32[128,512]{0,1:T(8,128)}, u32[]{:S(2)}) copy-start(f32[128,512]{0,1:T(8,128)} %copy.27) | copy-start | bytes 786436
  681.0 171.7 %copy-start.10 = (f32[128,512]{0,1:T(8,128)S(1)}, f32[128,512]{0,1:T(8,128)}, u32[]{:S(2)}) copy-start(f32[128,512]{0,1:T(8,128)} %copy.28) | copy-start | bytes 786436
  681.0 171.7 %copy-start.11 = (f32[128,512]{0,1:T(8,128)S(1)}, f32[128,512]{0,1:T(8,128)}, u32[]{:S(2)}) copy-start(f32[128,512]{0,1:T(8,128)} %copy.29) | copy-start | bytes 786436
  681.0 171.7 %copy-start.13 = (f32[128,512]{0,1:T(8,128)S(1)}, f32[128,512]{0,1:T(8,128)}, u32[]{:S(2)}) copy-start(f32[128,512]{0,1:T(8,128)} %copy-done.12) | copy-start | bytes 786436
  685.5 154.0 %collective-permute-start.2 = (f32[32,32]{1,0:T(8,128)S(1)}, f32[32,32]{1,0:T(8,128)S(1)}, u32[]{:S(2)}, u32[]{:S(2)}) collective-permute-start(f32[32,32]{1,0:T(8,128)S(1)} %convolution_subtract_fusion.20), channel_id=1, source_target_pairs={{0,8},{8,16},{16,24},{1,9},{9,17},{17,25},{2,10},{10,18},{18,26},{... | collective-permute-start | bytes 12296 | tf_op jit(solution)/shard_map/ppermute | solution.py:17
  847.2 49.3 %collective-permute-start.1 = (f32[32,4096]{1,0:T(8,128)S(1)}, f32[32,4096]{1,0:T(8,128)}, u32[]{:S(2)}, u32[]{:S(2)}) collective-permute-start(f32[32,4096]{1,0:T(8,128)S(1)} %convolution_subtract_fusion), channel_id=1, source_target_pairs={{0,8},{8,16},{16,24},{1,9},{9,17},{17,25},{2,10},{10,18},{18,26},{... | collective-permute-start | bytes 1572872 | tf_op jit(solution)/shard_map/ppermute | solution.py:17
  867.9 8.8 copy-start
  (14 other events, 64.8 us)
Sparse Core Ops, SparseCore 0:
  22.0 61.4 all-reduce.3
  230.4 81.0 all-gather.4
  336.3 58.1 all-reduce.5
  395.9 81.0 all-gather.8
  553.2 80.9 all-gather.10
  635.7 80.5 all-gather.6
where the time goes:
time: 926 us; the launch traced here: 914 us
  waiting for transfers between devices  350 us (38%)
  other arithmetic  271 us (29%)
  matrix products  189 us (20%)
  local copies, waits for them, and re-layouts  68.5 us (7%)
  between operations  20.9 us (2%)
  starting transfers between devices  14.1 us (2%)
    another operation x29, other arithmetic, local(): factor = jnp.linalg.cholesky(pivot_blk)  158 us
    ppermute x3, waiting for transfers between devices, shifted(): lax.ppermute(value, axis, [(source, source + steps) for source in range(l...  149 us
    dot_general x12, matrix products, outer_rows(): lax.dot_general(left_rows, right_rows, (((1,), (1,)), ((), ())), precisio...  134 us
    psum x2, waiting for transfers between devices, broadcast(): return lax.psum(block, axis)  89.8 us
    another operation x5, other arithmetic, solve_rows(): return jax.scipy.linalg.solve_triangular(factor, block.T, lower=True).T  79.9 us
    all_gather x2, waiting for transfers between devices, local(): factor_whole_a = lax.all_gather(factor_local_a, 'tile', axis=0, tiled=True)  73.9 us
    another operation x42, matrix products, solve_rows(): return jax.scipy.linalg.solve_triangular(factor, block.T, lower=True).T  47 us
    all_gather x2, waiting for transfers between devices, local(): factor_whole_c = lax.all_gather(factor_local_c, 'tile', axis=0, tiled=True)  37.2 us
  transfers between devices with their start and end apart: 9, of which 5 were waited for; matrix products, arithmetic and copies ran while one was open for 36% of the time, Pallas kernels for 0%

commit v1 on v0

--- a/solution.py
+++ b/solution.py
@@ -52,7 +52,32 @@
         )
         factor_local_c = solve_rows(factor, work_c[:, factor_offset:factor_ending])
         factor_whole_a = lax.all_gather(factor_local_a, "tile", axis=0, tiled=True)
-        factor_whole_c = lax.all_gather(factor_local_c, "tile", axis=0, tiled=True)
+        size, position, rows = (
+            lax.axis_size("tile"),
+            lax.axis_index("tile"),
+            factor_local_c.shape[0],
+        )
+        right = [(i, (i + 1) % size) for i in range(size)]
+        backward = [(i, (i - 1) % size) for i in range(size)]
+        factor_whole_c = jnp.zeros(
+            (*factor_local_c.shape[:0], size * rows, *factor_local_c.shape[0 + 1 :]),
+            factor_local_c.dtype,
+        )
+        factor_whole_c = lax.dynamic_update_slice_in_dim(
+            factor_whole_c, factor_local_c, position * rows, axis=0
+        )
+        from_left = from_right = factor_local_c
+        halfway = size // 2
+        for step in range(1, halfway + 1):
+            from_left = lax.ppermute(from_left, "tile", right)
+            factor_whole_c = lax.dynamic_update_slice_in_dim(
+                factor_whole_c, from_left, (position - step) % size * rows, axis=0
+            )
+            if step < size - halfway:
+                from_right = lax.ppermute(from_right, "tile", backward)
+                factor_whole_c = lax.dynamic_update_slice_in_dim(
+                    factor_whole_c, from_right, (position + step) % size * rows, axis=0
+                )
         factor_local_r = solve_rows(factor, arrow_a[:, factor_offset:factor_ending])
         panel_k = (
             factor_offset,

time: 926 us -> 1080 us (1.17)
  waiting for transfers between devices: 350 us -> 472 us
  local copies, waits for them, and re-layouts: 68.5 us -> 88.6 us
  starting transfers between devices: 14.1 us -> 30.8 us
    ppermute x0 -> x14, waiting for transfers between devices: none -> 178 us  [the longest x8 171 us: local(): from_left = lax.ppermute(from_left, 'tile', right)]
    all_gather x2 -> x0, waiting for transfers between devices: 37.2 us -> none  [local(): factor_whole_c = lax.all_gather(factor_local_c, 'tile', axis=0, tiled=True)]
    all_gather x2, waiting for transfers between devices: 73.9 us -> 51 us  [local(): factor_whole_a = lax.all_gather(factor_local_a, 'tile', axis=0, tiled=True)]
    dynamic_update_slice x0 -> x14, local copies, waits for them, and re-layouts: none -> 21.3 us  [the longest x8 11.8 us: local(): lax.dynamic_update_slice_in_dim(factor_whole_c, from_left, (position - st...]
    ppermute x0 -> x14, starting transfers between devices: none -> 19.7 us  [the longest x6 19.4 us: local(): from_right = lax.ppermute(from_right, 'tile', backward)]
    unnamed x64 -> x66, local copies, waits for them, and re-layouts: 30.9 us -> 30 us
  transfers between devices with their start and end apart: 9 -> 21, of which waited for: 5 -> 13; matrix products, arithmetic and copies ran while one was open for 36% -> 30% of each run, Pallas kernels for 0% -> 0%
where the time goes in v1:
time: 1080 us; the launch traced here: 1070 us
  waiting for transfers between devices  472 us (44%)
  other arithmetic  271 us (25%)
  matrix products  185 us (17%)
  local copies, waits for them, and re-layouts  88.6 us (8%)
  starting transfers between devices  30.8 us (3%)
  between operations  20.6 us (2%)
    ppermute x8, waiting for transfers between devices, local(): from_left = lax.ppermute(from_left, 'tile', right)  171 us
    another operation x29, other arithmetic, local(): factor = jnp.linalg.cholesky(pivot_blk)  158 us
    ppermute x3, waiting for transfers between devices, shifted(): lax.ppermute(value, axis, [(source, source + steps) for source in range(l...  146 us
    dot_general x12, matrix products, outer_rows(): lax.dot_general(left_rows, right_rows, (((1,), (1,)), ((), ())), precisio...  133 us
    psum x2, waiting for transfers between devices, broadcast(): return lax.psum(block, axis)  97.4 us
    another operation x5, other arithmetic, solve_rows(): return jax.scipy.linalg.solve_triangular(factor, block.T, lower=True).T  79.9 us
    all_gather x2, waiting for transfers between devices, local(): factor_whole_a = lax.all_gather(factor_local_a, 'tile', axis=0, tiled=True)  51 us
    another operation x42, matrix products, solve_rows(): return jax.scipy.linalg.solve_triangular(factor, block.T, lower=True).T  44 us
  transfers between devices with their start and end apart: 21, of which 13 were waited for; matrix products, arithmetic and copies ran while one was open for 30% of the time, Pallas kernels for 0%

profile of v1, /device:TPU:0, one launch (start us, length us, event | category | flops | bytes accessed | tf_op | source)
XLA Modules:
  0.0 1067.5 jit_solution(4053819786562536089)
XLA Ops:
  22.5 61.0 %all-reduce.4.cloned.1.call-done = f32[512,512]{1,0:T(8,128)} async-done(((f32[512,512]{1,0:T(8,128)}), f32[512,512]{1,0:T(8,128)}) %all-reduce.4.cloned.1.call-update) | async-done | bytes 1048592 | tf_op jit(solution)/shard_map/psum | solution.py:11
  86.6 11.7 %cholesky.286 = f32[128,128]{1,0:T(8,128)S(1)} custom-call(f32[128,128]{1,0:T(8,128)S(1)} %copy.14), custom_call_target="Cholesky" | custom-call | tf_op jit(solution)/shard_map/jit(cholesky)/cholesky | solution.py:47
  109.3 11.7 %cholesky.305 = f32[128,128]{1,0:T(8,128)S(1)} custom-call(f32[128,128]{1,0:T(8,128)S(1)} %copy.16), custom_call_target="Cholesky" | custom-call | tf_op jit(solution)/shard_map/jit(cholesky)/cholesky | solution.py:47
  132.0 11.7 %cholesky.326 = f32[128,128]{1,0:T(8,128)S(1)} custom-call(f32[128,128]{1,0:T(8,128)S(1)} %copy.18), custom_call_target="Cholesky" | custom-call | tf_op jit(solution)/shard_map/jit(cholesky)/cholesky | solution.py:47
  155.0 12.1 %cholesky.343 = f32[128,128]{1,0:T(8,128)S(1)} custom-call(f32[128,128]{1,0:T(8,128)S(1)} %copy.20), custom_call_target="Cholesky" | custom-call | tf_op jit(solution)/shard_map/jit(cholesky)/cholesky | solution.py:47
  179.3 39.3 %custom-call.36 = f32[4,128,128]{1,2,0:T(8,128)S(1)} custom-call(f32[4,128,128]{2,1,0:T(8,128)S(1)} %get-tuple-element.193), custom_call_target="InvertDiagBlocksLowerTriangular" | custom-call | tf_op jit(solution)/shard_map/jit(_solve_triangular)/triangular_solve | solution.py:31
  254.4 37.9 %collective-permute-done = f32[512,512]{1,0:T(8,128)} collective-permute-done((f32[512,512]{1,0:T(8,128)}, f32[512,512]{1,0:T(8,128)}, u32[]{:S(2)}, u32[]{:S(2)}) %collective-permute-start) | collective-permute-done | bytes 1048608 | tf_op jit(solution)/shard_map/ppermute | solution.py:72
  292.4 51.0 %all-gather.3.cloned.1.call-done = f32[4096,512]{1,0:T(8,128)} async-done(((f32[512,512]{1,0:T(8,128)}), f32[4096,512]{1,0:T(8,128)}) %all-gather.3.cloned.1.call-update) | async-done | bytes 8388624 | tf_op jit(solution)/shard_map/all_gather | solution.py:54
  343.5 17.5 %constant_dynamic-update-slice_fusion.20 = (f32[512,4096]{1,0:T(8,128)}, f32[512,3584]{1,0:T(8,128)S(1)}) fusion(f32[512,4096]{1,0:T(8,128)} %get-tuple-element.217, f32[4096,512]{1,0:T(8,128)} %all-gather.3.cloned.1.call-done, f32[128,512]{0,1:T(8,128)S(1)} %copy-done.20, f32[128,512]{0,1:T(8,128)S(1)} %copy.23, f32[128,512]{0,1:T(8,128)S(1)} %copy-done.16, ...), kind=kOutput, calls=%fused_computation.261 | convolution fusion | flops 11280842752 | bytes 30409728 | tf_op jit(solution)/shard_map/dot_general | solution.py:21
  367.9 17.7 %constant_dynamic-update-slice_fusion.19 = (f32[512,4096]{1,0:T(8,128)}, f32[512,3584]{1,0:T(8,128)S(1)}) fusion(f32[512,4096]{1,0:T(8,128)} %get-tuple-element.230, f32[4096,512]{1,0:T(8,128)} %all-gather.3.cloned.1.call-done, f32[128,512]{0,1:T(8,128)S(1)} %fusion.132, f32[128,512]{0,1:T(8,128)S(1)} %copy.33, f32[128,512]{0,1:T(8,128)S(1)} %copy.32, ...), kind=kOutput, calls=%fused_computation.260 | convolution fusion | flops 11278745600 | bytes 30408704 | tf_op jit(solution)/shard_map/dot_general | solution.py:21
  389.6 36.4 %all-reduce.6.cloned.1.call-done = f32[512,512]{0,1:T(8,128)} async-done(((f32[512,512]{0,1:T(8,128)}), f32[512,512]{0,1:T(8,128)}) %all-reduce.6.cloned.1.call-update) | async-done | bytes 1048592 | tf_op jit(solution)/shard_map/psum | solution.py:11
  430.0 11.7 %cholesky.358 = f32[128,128]{1,0:T(8,128)S(1)} custom-call(f32[128,128]{1,0:T(8,128)S(1)} %cholesky.439), custom_call_target="Cholesky" | custom-call | tf_op jit(solution)/shard_map/jit(cholesky)/cholesky | solution.py:47
  454.3 11.7 %cholesky.377 = f32[128,128]{1,0:T(8,128)S(1)} custom-call(f32[128,128]{1,0:T(8,128)S(1)} %cholesky.443), custom_call_target="Cholesky" | custom-call | tf_op jit(solution)/shard_map/jit(cholesky)/cholesky | solution.py:47
  518.9 12.0 %while.25 = (s32[]{:T(128)}, f32[512,512]{1,0:T(8,128)}, s32[4,2]{0,1:T(2,128)S(1)}, f32[4,128,128]{2,1,0:T(8,128)S(1)}, s32[]{:T(128)}) while((s32[]{:T(128)}, f32[512,512]{1,0:T(8,128)}, s32[4,2]{0,1:T(2,128)S(1)}, f32[4,128,128]{2,1,0:T(8,128)S(1)}, s32[]{:T(128)}) %tuple.141), condition=%wide.while_cond.12.clone, body=%wide.while_body.12.clone.sunk | while | flops 2 | bytes 131181 | solution.py:31
  531.0 39.3 %custom-call.40 = f32[4,128,128]{1,2,0:T(8,128)S(1)} custom-call(f32[4,128,128]{2,1,0:T(8,128)S(1)} %get-tuple-element.194), custom_call_target="InvertDiagBlocksLowerTriangular" | custom-call | tf_op jit(solution)/shard_map/jit(_solve_triangular)/triangular_solve | solution.py:31
  607.5 38.9 %collective-permute-done.7 = f32[512,512]{1,0:T(8,128)} collective-permute-done((f32[512,512]{1,0:T(8,128)S(1)}, f32[512,512]{1,0:T(8,128)}, u32[]{:S(2)}, u32[]{:S(2)}) %collective-permute-start.7) | collective-permute-done | bytes 1048608 | tf_op jit(solution)/shard_map/ppermute | solution.py:72
  653.1 38.2 %collective-permute-done.4 = f32[512,512]{1,0:T(8,128)} collective-permute-done((f32[512,512]{1,0:T(8,128)}, f32[512,512]{1,0:T(8,128)}, u32[]{:S(2)}, u32[]{:S(2)}) %collective-permute-start.4) | collective-permute-done | bytes 1048608 | tf_op jit(solution)/shard_map/ppermute | solution.py:72
  707.1 29.2 %collective-permute-done.9 = f32[512,512]{1,0:T(8,128)} collective-permute-done((f32[512,512]{1,0:T(8,128)}, f32[512,512]{1,0:T(8,128)}, u32[]{:S(2)}, u32[]{:S(2)}) %collective-permute-start.9) | collective-permute-done | bytes 1048608 | tf_op jit(solution)/shard_map/ppermute | solution.py:72
  741.3 20.8 %collective-permute-done.6 = f32[512,512]{1,0:T(8,128)} collective-permute-done((f32[512,512]{1,0:T(8,128)}, f32[512,512]{1,0:T(8,128)}, u32[]{:S(2)}, u32[]{:S(2)}) %collective-permute-start.6) | collective-permute-done | bytes 1048608 | tf_op jit(solution)/shard_map/ppermute | solution.py:72
  765.2 17.3 %fusion.94 = f32[512,4096]{1,0:T(8,128)} fusion(f32[4096,512]{1,0:T(8,128)} %constant_dynamic-update-slice_fusion.10, f32[128,512]{0,1:T(8,128)S(1)} %fusion.132, f32[128,512]{0,1:T(8,128)S(1)} %copy.33, f32[128,512]{0,1:T(8,128)S(1)} %copy.32, f32[128,512]{0,1:T(8,128)S(1)} %copy.31), kind=kOutput, calls=%fused_computation.137 | convolution fusion | flops 12885688320 | bytes 17825792 | tf_op jit(solution)/shard_map/dot_general | solution.py:21
  798.7 18.2 %subtract_subtract_fusion = f32[512,4096]{1,0:T(8,128)} fusion(f32[512,4096]{1,0:T(8,128)} %param.37, f32[512,4096]{1,0:T(8,128)} %fusion.94, f32[4096,512]{1,0:T(8,128)S(1)} %constant_dynamic-update-slice_fusion.2, f32[128,512]{0,1:T(8,128)S(1)} %fusion.142, f32[128,512]{0,1:T(8,128)S(1)} %copy.37, f32[128,512]{0,1:T(8,128)S(1)} %copy.36, ...), kind=kOutput, calls=%fused_computation.4 | convolution fusion | flops 12889882624 | bytes 34603008 | tf_op jit(solution)/shard_map/dot_general | solution.py:21
  861.6 145.7 %collective-permute-done.16 = f32[32,32]{1,0:T(8,128)S(1)} collective-permute-done((f32[32,32]{1,0:T(8,128)S(1)}, f32[32,32]{1,0:T(8,128)S(1)}, u32[]{:S(2)}, u32[]{:S(2)}) %collective-permute-start.16) | collective-permute-done | bytes 4128 | tf_op jit(solution)/shard_map/ppermute | solution.py:17
  1007.4 15.4 %fusion.7 = f32[512,4096]{1,0:T(8,128)} fusion(f32[512,4096]{1,0:T(8,128)} %get-tuple-element.215, f32[4096,512]{1,0:T(8,128)} %all-gather.5.cloned.1.call-done, pred[512]{0:T(512)(128)(4,1)S(1)} %fusion.168, f32[128,512]{0,1:T(8,128)S(1)} %copy-done.14, f32[128,512]{0,1:T(8,128)S(1)} %copy-done.9, f32[128,512]{0,1:T(8,128)S(1)} %copy-done.10, ...), kind=kOutput, calls=%fused_computation.17 | convolution fusion | flops 9669443584 | bytes 19923968 | tf_op jit(solution)/shard_map/dot_general | solution.py:21
  1037.4 14.0 %fusion.6 = f32[512,4096]{1,0:T(8,128)} fusion(f32[512,4096]{1,0:T(8,128)} %get-tuple-element.228, f32[4096,512]{1,0:T(8,128)S(1)} %copy-done, f32[128,512]{0,1:T(8,128)S(1)} %fusion.142, f32[128,512]{0,1:T(8,128)S(1)} %copy.37, f32[128,512]{0,1:T(8,128)S(1)} %copy.36, f32[128,512]{0,1:T(8,128)S(1)} %copy.35), kind=kOutput, calls=%fused_computation.15 | convolution fusion | flops 9667608576 | bytes 19922944 | tf_op jit(solution)/shard_map/dot_general | solution.py:21
  (285 shorter events, 346.6 us)
Async XLA Ops:
  7.2 76.3 %all-reduce.4.cloned.1.call-start = ((), (), s32[]{:S(2)}) async-start(), calls=%async_computation | async-start | bytes 2097152 | tf_op jit(solution)/shard_map/psum | solution.py:11
  21.8 321.6 %all-gather.3.cloned.1.call-start = ((), (), s32[]{:S(2)}) async-start(), calls=%async_computation.1 | async-start | bytes 9437184 | tf_op jit(solution)/shard_map/all_gather | solution.py:54
  229.0 197.0 %all-reduce.6.cloned.1.call-start = ((), (), s32[]{:S(2)}) async-start(), calls=%async_computation.2 | async-start | bytes 2097152 | tf_op jit(solution)/shard_map/psum | solution.py:11
  242.3 49.9 %collective-permute-start = (f32[512,512]{1,0:T(8,128)}, f32[512,512]{1,0:T(8,128)}, u32[]{:S(2)}, u32[]{:S(2)}) collective-permute-start(f32[512,512]{1,0:T(8,128)} %fusion.95), channel_id=1, source_target_pairs={{0,1},{1,2},{2,3},{3,4},{4,5},{5,6},{6,7},{7,0},{8,9},{9,10},{10,1... | collective-permute-start | bytes 3145736 | tf_op jit(solution)/shard_map/ppermute | solution.py:72
  243.0 356.9 %collective-permute-start.1 = (f32[512,512]{1,0:T(8,128)}, f32[512,512]{1,0:T(8,128)}, u32[]{:S(2)}, u32[]{:S(2)}) collective-permute-start(f32[512,512]{1,0:T(8,128)} %fusion.95), channel_id=1, source_target_pairs={{0,7},{1,0},{2,1},{3,2},{4,3},{5,4},{6,5},{7,6},{8,15},{9,8},{10,9... | collective-permute-start | bytes 3145736 | tf_op jit(solution)/shard_map/ppermute | solution.py:77
  292.2 311.3 %collective-permute-start.2 = (f32[512,512]{1,0:T(8,128)}, f32[512,512]{1,0:T(8,128)}, u32[]{:S(2)}, u32[]{:S(2)}) collective-permute-start(f32[512,512]{1,0:T(8,128)} %collective-permute-done), channel_id=1, source_target_pairs={{0,1},{1,2},{2,3},{3,4},{4,5},{5,6},{6,7},{7,0},{8,9},{9,10},{10,1... | collective-permute-start | bytes 3145736 | tf_op jit(solution)/shard_map/ppermute | solution.py:72
  367.6 639.7 %all-gather.5.cloned.1.call-start = ((), (), s32[]{:S(2)}) async-start(), calls=%async_computation.3 | async-start | bytes 9437184 | tf_op jit(solution)/shard_map/all_gather | solution.py:54
  599.9 46.4 %collective-permute-start.7 = (f32[512,512]{1,0:T(8,128)S(1)}, f32[512,512]{1,0:T(8,128)}, u32[]{:S(2)}, u32[]{:S(2)}) collective-permute-start(f32[512,512]{1,0:T(8,128)S(1)} %fusion.93), channel_id=1, source_target_pairs={{0,1},{1,2},{2,3},{3,4},{4,5},{5,6},{6,7},{7,0},{8,9},{9,10},{10,1... | collective-permute-start | bytes 3145736 | tf_op jit(solution)/shard_map/ppermute | solution.py:72
  600.0 49.4 %collective-permute-start.3 = (f32[512,512]{1,0:T(8,128)}, f32[512,512]{1,0:T(8,128)}, u32[]{:S(2)}, u32[]{:S(2)}) collective-permute-start(f32[512,512]{1,0:T(8,128)} %collective-permute-done.1), channel_id=1, source_target_pairs={{0,7},{1,0},{2,1},{3,2},{4,3},{5,4},{6,5},{7,6},{8,15},{9,8},{10,9... | collective-permute-start | bytes 3145736 | tf_op jit(solution)/shard_map/ppermute | solution.py:77
  603.5 87.8 %collective-permute-start.4 = (f32[512,512]{1,0:T(8,128)}, f32[512,512]{1,0:T(8,128)}, u32[]{:S(2)}, u32[]{:S(2)}) collective-permute-start(f32[512,512]{1,0:T(8,128)} %collective-permute-done.2), channel_id=1, source_target_pairs={{0,1},{1,2},{2,3},{3,4},{4,5},{5,6},{6,7},{7,0},{8,9},{9,10},{10,1... | collective-permute-start | bytes 3145736 | tf_op jit(solution)/shard_map/ppermute | solution.py:72
  603.5 90.7 %collective-permute-start.8 = (f32[512,512]{1,0:T(8,128)S(1)}, f32[512,512]{1,0:T(8,128)}, u32[]{:S(2)}, u32[]{:S(2)}) collective-permute-start(f32[512,512]{1,0:T(8,128)S(1)} %fusion.93), channel_id=1, source_target_pairs={{0,7},{1,0},{2,1},{3,2},{4,3},{5,4},{6,5},{7,6},{8,15},{9,8},{10,9... | collective-permute-start | bytes 3145736 | tf_op jit(solution)/shard_map/ppermute | solution.py:77
  646.3 89.9 %collective-permute-start.9 = (f32[512,512]{1,0:T(8,128)}, f32[512,512]{1,0:T(8,128)}, u32[]{:S(2)}, u32[]{:S(2)}) collective-permute-start(f32[512,512]{1,0:T(8,128)} %collective-permute-done.7), channel_id=1, source_target_pairs={{0,1},{1,2},{2,3},{3,4},{4,5},{5,6},{6,7},{7,0},{8,9},{9,10},{10,1... | collective-permute-start | bytes 3145736 | tf_op jit(solution)/shard_map/ppermute | solution.py:72
  649.4 89.7 %collective-permute-start.5 = (f32[512,512]{1,0:T(8,128)}, f32[512,512]{1,0:T(8,128)}, u32[]{:S(2)}, u32[]{:S(2)}) collective-permute-start(f32[512,512]{1,0:T(8,128)} %collective-permute-done.3), channel_id=1, source_target_pairs={{0,7},{1,0},{2,1},{3,2},{4,3},{5,4},{6,5},{7,6},{8,15},{9,8},{10,9... | collective-permute-start | bytes 3145736 | tf_op jit(solution)/shard_map/ppermute | solution.py:77
  691.3 70.8 %collective-permute-start.6 = (f32[512,512]{1,0:T(8,128)}, f32[512,512]{1,0:T(8,128)}, u32[]{:S(2)}, u32[]{:S(2)}) collective-permute-start(f32[512,512]{1,0:T(8,128)} %collective-permute-done.4), channel_id=1, source_target_pairs={{0,1},{1,2},{2,3},{3,4},{4,5},{5,6},{6,7},{7,0},{8,9},{9,10},{10,1... | collective-permute-start | bytes 3145736 | tf_op jit(solution)/shard_map/ppermute | solution.py:72
  694.2 70.2 %collective-permute-start.10 = (f32[512,512]{1,0:T(8,128)}, f32[512,512]{1,0:T(8,128)}, u32[]{:S(2)}, u32[]{:S(2)}) collective-permute-start(f32[512,512]{1,0:T(8,128)} %collective-permute-done.8), channel_id=1, source_target_pairs={{0,7},{1,0},{2,1},{3,2},{4,3},{5,4},{6,5},{7,6},{8,15},{9,8},{10,9... | collective-permute-start | bytes 3145736 | tf_op jit(solution)/shard_map/ppermute | solution.py:77
  736.2 46.3 %collective-permute-start.11 = (f32[512,512]{1,0:T(8,128)}, f32[512,512]{1,0:T(8,128)S(1)}, u32[]{:S(2)}, u32[]{:S(2)}) collective-permute-start(f32[512,512]{1,0:T(8,128)} %collective-permute-done.9), channel_id=1, source_target_pairs={{0,1},{1,2},{2,3},{3,4},{4,5},{5,6},{6,7},{7,0},{8,9},{9,10},{10,1... | collective-permute-start | bytes 3145736 | tf_op jit(solution)/shard_map/ppermute | solution.py:72
  764.4 27.6 %collective-permute-start.12 = (f32[512,512]{1,0:T(8,128)}, f32[512,512]{1,0:T(8,128)S(1)}, u32[]{:S(2)}, u32[]{:S(2)}) collective-permute-start(f32[512,512]{1,0:T(8,128)} %collective-permute-done.10), channel_id=1, source_target_pairs={{0,7},{1,0},{2,1},{3,2},{4,3},{5,4},{6,5},{7,6},{8,15},{9,8},{10,9... | collective-permute-start | bytes 3145736 | tf_op jit(solution)/shard_map/ppermute | solution.py:77
  782.5 16.0 %collective-permute-start.13 = (f32[512,512]{1,0:T(8,128)S(1)}, f32[512,512]{1,0:T(8,128)S(1)}, u32[]{:S(2)}, u32[]{:S(2)}) collective-permute-start(f32[512,512]{1,0:T(8,128)S(1)} %collective-permute-done.11), channel_id=1, source_target_pairs={{0,1},{1,2},{2,3},{3,4},{4,5},{5,6},{6,7},{7,0},{8,9},{9,10},{10,1... | collective-permute-start | bytes 3145736 | tf_op jit(solution)/shard_map/ppermute | solution.py:72
  816.8 190.5 %collective-permute-start.14 = (f32[512,4096]{1,0:T(8,128)}, f32[512,4096]{1,0:T(8,128)}, u32[]{:S(2)}, u32[]{:S(2)}) collective-permute-start(f32[512,4096]{1,0:T(8,128)} %subtract_subtract_fusion), channel_id=1, source_target_pairs={{0,8},{8,16},{16,24},{1,9},{9,17},{17,25},{2,10},{10,18},{18,26},{... | collective-permute-start | bytes 25165832 | tf_op jit(solution)/shard_map/ppermute | solution.py:17
  839.4 167.9 %copy-start.9 = (f32[128,512]{0,1:T(8,128)S(1)}, f32[128,512]{0,1:T(8,128)}, u32[]{:S(2)}) copy-start(f32[128,512]{0,1:T(8,128)} %copy-done.8) | copy-start | bytes 786436
  839.5 167.9 %copy-start.10 = (f32[128,512]{0,1:T(8,128)S(1)}, f32[128,512]{0,1:T(8,128)}, u32[]{:S(2)}) copy-start(f32[128,512]{0,1:T(8,128)} %copy.28) | copy-start | bytes 786436
  839.5 167.9 %copy-start.12 = (f32[128,512]{0,1:T(8,128)S(1)}, f32[128,512]{0,1:T(8,128)}, u32[]{:S(2)}) copy-start(f32[128,512]{0,1:T(8,128)} %copy-done.11) | copy-start | bytes 786436
  857.2 150.1 %collective-permute-start.15 = (f32[32,4096]{1,0:T(8,128)S(1)}, f32[32,4096]{1,0:T(8,128)S(1)}, u32[]{:S(2)}, u32[]{:S(2)}) collective-permute-start(f32[32,4096]{1,0:T(8,128)S(1)} %fusion.18), channel_id=1, source_target_pairs={{0,8},{8,16},{16,24},{1,9},{9,17},{17,25},{2,10},{10,18},{18,26},{... | collective-permute-start | bytes 1572872 | tf_op jit(solution)/shard_map/ppermute | solution.py:17
  858.8 148.6 %collective-permute-start.16 = (f32[32,32]{1,0:T(8,128)S(1)}, f32[32,32]{1,0:T(8,128)S(1)}, u32[]{:S(2)}, u32[]{:S(2)}) collective-permute-start(f32[32,32]{1,0:T(8,128)S(1)} %convolution_subtract_fusion.19), channel_id=1, source_target_pairs={{0,8},{8,16},{16,24},{1,9},{9,17},{17,25},{2,10},{10,18},{18,26},{... | collective-permute-start | bytes 12296 | tf_op jit(solution)/shard_map/ppermute | solution.py:17
  (27 other events, 712.0 us)
Sparse Core Ops, SparseCore 0:
  22.0 61.4 all-reduce.3
  229.1 114.3 all-gather.2
  367.7 58.2 all-reduce.5
  596.1 142.6 all-gather.4
